TPU v7x, 512 devices: a whole 4x4x16 slice. The times are simulated.
512 devices in a mesh: seq: 16 (over z), exp: 32 (over y, x, core).
Axes of the slice: x: 4, y: 4, z: 16, core: 2. Of those that a mesh axis runs over, the one named last changes fastest.
Arguments:
- byte_embed: bfloat16 [32, 2048, 1024], P('exp', 'seq'), may hold values from -16 to 16
- score_weight: float32 [1024], replicated, may hold values from -1 to 1
- norm_gain: float32 [1024], replicated, may hold values from 0.25 to 1.75
- router: bfloat16 [1024, 32], replicated, may hold values from -0.1875 to 0.1875
- routes: int32 [32, 512, 2], P('exp', 'seq'), may hold values from 0 to 31, all different within a row; in each aligned block of 32 rows (0 to 31, 32 to 63, ..., all dimensions but the last counted through in order) at most 3 rows name the same one
- expert_in: bfloat16 [32, 1024, 4096], P('exp', None, 'seq'), may hold values from -0.1875 to 0.1875
- expert_out: bfloat16 [32, 4096, 1024], P('exp', 'seq'), may hold values from -0.09375 to 0.09375
- cotangent: bfloat16 [32, 512, 1024], P('exp', 'seq'), may hold values from -6 to 6
Outputs:
- grad_embed: bfloat16 [32, 2048, 1024], P('exp', 'seq')
- grad_in: float32 [32, 1024, 4096], P('exp', None, 'seq')
- grad_out: float32 [32, 4096, 1024], P('exp', 'seq')
Inputs may be any that keep to these rules, and one draw needn't show every extreme that they name: `routes`: among the 32 tokens of one device, at most 3 pairs name the same expert, and some device reaches 3 for some expert. The two experts of a token differ.
All inputs are finite; a program needn't handle non-finite values.
Results may differ from a plain program's by a relative error of at most 0.014.
Values may be sent and summed in bfloat16 or wider, within the bound.
A program may use at most 64 MiB of HBM per device.

v0:
```python
import jax
import jax.numpy as jnp
from jax import lax
from jax.sharding import PartitionSpec as P

SQRT_HALF = 0.7071067811865476
INV_ROOT_TWO_PI = 0.3989422804014327


def front(inputs, norm_gain, score_weight, router, routes):
    batches, length, features = inputs.shape
    highest = lax.Precision.HIGHEST
    quartets = inputs.reshape(batches, length // 4, 4, features)
    pair_means = quartets.reshape(batches, length // 4, 2, 2, features).mean(axis=3)
    quad_mean = quartets.mean(axis=2)
    score_one = jnp.einsum("btqd,d->btq", quartets, score_weight, precision=highest)
    score_two = jnp.repeat(
        jnp.einsum("btpd,d->btp", pair_means, score_weight, precision=highest), 2, axis=2
    )
    score_four = jnp.broadcast_to(
        jnp.einsum("btd,d->bt", quad_mean, score_weight, precision=highest)[:, :, None],
        score_one.shape,
    )
    largest = jnp.maximum(jnp.maximum(score_one, score_two), score_four)
    weight_one = jnp.exp(score_one - largest)
    weight_two = jnp.exp(score_two - largest)
    weight_four = jnp.exp(score_four - largest)
    denominator = weight_one + weight_two + weight_four
    pair_full = jnp.repeat(pair_means, 2, axis=2)
    blended = (
        weight_one[..., None] * quartets
        + weight_two[..., None] * pair_full
        + weight_four[..., None] * quad_mean[:, :, None, :]
    ) / denominator[..., None]
    tokens = blended.mean(axis=2)
    mean_square = jnp.mean(tokens * tokens, axis=-1, keepdims=True)
    normed = tokens * lax.rsqrt(mean_square + 1e-06) * norm_gain
    logits = jnp.einsum("btd,de->bte", normed, router.astype(jnp.float32), precision=highest)
    experts = logits.shape[-1]
    sigmoid_all = 1.0 / (1.0 + jnp.exp(-logits))
    chosen = (routes[..., None] == jnp.arange(experts, dtype=jnp.int32)).astype(jnp.float32)
    picked = jnp.sum(chosen * sigmoid_all[:, :, None, :], axis=-1)
    gate_values = picked / jnp.sum(picked, axis=-1, keepdims=True)
    return (tokens, normed, gate_values)


def deliver(row_stack, gates_in):
    owned_rows, owned_gates = (
        lax.all_to_all(row_stack, "exp", split_axis=1, concat_axis=1, tiled=True),
        lax.all_to_all(gates_in, "exp", split_axis=1, concat_axis=1, tiled=True),
    )
    return (
        lax.all_gather(owned_rows, "seq", axis=1, tiled=True),
        lax.all_gather(owned_gates, "seq", axis=1, tiled=True),
    )


def per_device(
    byte_embed, score_weight, norm_gain, router, routes, expert_in, expert_out, cotangent
):
    experts_all = router.shape[1]
    token_count = routes.shape[1]
    width_model = byte_embed.shape[2]
    capacity = max(2, 3 * token_count // experts_all)
    owners = lax.axis_size("exp")
    slot_count = lax.axis_size("seq") * owners * capacity
    highest = lax.Precision.HIGHEST
    contract_rows = (((0,), (0,)), ((), ()))
    contract_cols = (((1,), (1,)), ((), ()))

    def local_front(values):
        return front(values, norm_gain, score_weight, router, routes)

    (tokens, normed, gate_values), pullback = jax.vjp(local_front, byte_embed.astype(jnp.float32))
    normed_rows = normed[0].astype(jnp.bfloat16)
    route_rows = routes[0]
    onehot = (route_rows[:, :, None] == jnp.arange(experts_all, dtype=jnp.int32)).astype(jnp.int32)
    running = jnp.cumsum(onehot.reshape(2 * token_count, experts_all), axis=0)
    running = running.reshape(token_count, 2, experts_all)
    position = jnp.sum(onehot * (running - 1), axis=2)
    slot_index = route_rows * capacity + position
    matches = (
        slot_index[:, :, None] == jnp.arange(experts_all * capacity, dtype=jnp.int32)
    ).astype(jnp.float32)
    picker = jnp.sum(matches, axis=1).astype(jnp.bfloat16)
    token_buffer = lax.dot_general(
        picker, normed_rows, contract_rows, preferred_element_type=jnp.float32
    )
    cot_buffer = lax.dot_general(
        picker, cotangent[0], contract_rows, preferred_element_type=jnp.float32
    )
    row_buffer = (
        jnp.stack([token_buffer, cot_buffer])
        .astype(jnp.bfloat16)
        .reshape(2, experts_all, capacity, width_model)
    )
    gate_buffer = jnp.einsum("tks,tk->s", matches, gate_values[0], precision=highest)
    gate_buffer = gate_buffer.astype(jnp.bfloat16).reshape(1, experts_all, capacity)
    weight_in = expert_in[0]
    weight_out = expert_out[0]
    both_rows, slot_gates = deliver(row_buffer, gate_buffer)
    token_rows = both_rows[0].reshape(slot_count, width_model)
    cot_rows = both_rows[1].reshape(slot_count, width_model)
    gate_first = slot_gates.reshape(slot_count).astype(jnp.float32)
    preact = jnp.dot(token_rows, weight_in, preferred_element_type=jnp.float32)
    normal_cdf = 0.5 * (1.0 + jax.scipy.special.erf(preact * SQRT_HALF))
    normal_pdf = INV_ROOT_TWO_PI * jnp.exp(-0.5 * preact * preact)
    hidden = preact * normal_cdf
    upstream = lax.dot_general(
        cot_rows, weight_out, contract_cols, preferred_element_type=jnp.float32
    )
    gate_terms = jnp.sum(hidden * upstream, axis=1)
    hidden_grad = (gate_first[:, None] * upstream * (normal_cdf + preact * normal_pdf)).astype(
        jnp.bfloat16
    )
    gated_hidden = (gate_first[:, None] * hidden).astype(jnp.bfloat16)
    grad_out = lax.dot_general(
        gated_hidden, cot_rows, contract_rows, preferred_element_type=jnp.float32
    )
    grad_in = lax.dot_general(
        token_rows, hidden_grad, contract_rows, preferred_element_type=jnp.float32
    )
    own_slots = owners * capacity
    summed_rows = lax.psum_scatter(
        lax.dot_general(
            hidden_grad, weight_in, contract_cols, preferred_element_type=jnp.float32
        ).astype(jnp.bfloat16),
        "seq",
        scatter_dimension=0,
        tiled=True,
    )
    every_term = lax.psum(gate_terms, "seq")
    own_terms = lax.dynamic_slice_in_dim(
        every_term, lax.axis_index("seq") * own_slots, own_slots, 0
    )
    returned_rows, returned_gates = (
        lax.all_to_all(
            summed_rows.reshape(owners, capacity, width_model),
            "exp",
            split_axis=0,
            concat_axis=0,
            tiled=True,
        ),
        lax.all_to_all(
            own_terms.astype(jnp.bfloat16).reshape(owners, capacity),
            "exp",
            split_axis=0,
            concat_axis=0,
            tiled=True,
        ),
    )
    normed_grad = jnp.dot(
        picker,
        returned_rows.reshape(experts_all * capacity, width_model),
        preferred_element_type=jnp.float32,
    )
    gate_grad = jnp.einsum(
        "tks,s->tk", matches, returned_gates.reshape(-1).astype(jnp.float32), precision=highest
    )
    (embed_grad,) = pullback((cotangent.astype(jnp.float32), normed_grad[None], gate_grad[None]))
    return (embed_grad.astype(jnp.bfloat16), grad_in[None], grad_out[None])


def solution(mesh):
    in_specs = (
        P("exp", "seq", None),
        P(),
        P(),
        P(),
        P("exp", "seq", None),
        P("exp", None, "seq"),
        P("exp", "seq", None),
        P("exp", "seq", None),
    )
    out_specs = (P("exp", "seq", None), P("exp", None, "seq"), P("exp", "seq", None))
    return jax.shard_map(
        per_device, mesh=mesh, in_specs=in_specs, out_specs=out_specs, check_vma=False
    )
```

profile of v0, /device:TPU:1, one launch (start us, length us, event | category | flops | bytes accessed | tf_op | source)
XLA Modules:
  0.0 291.5 jit_solution(9137847497761137692)
XLA Ops:
  7.2 1.4 reshape.708
  8.6 1.1 reshape.709
  10.0 0.8 reduce_sum.182
  11.0 0.6 fusion.53
  11.7 0.3 reduce_sum.183
  12.0 0.2 convolution_bitcast_fusion.3
  12.2 0.7 fusion.22
  13.0 0.3 broadcast_in_dim.93
  13.3 0.5 broadcast_in_dim.94
  13.9 1.1 fusion.21
  15.2 0.5 fusion.49
  16.7 0.2 convolution_convert_fusion.2
  17.3 0.2 fusion.6
  17.5 0.4 copy.132
  18.0 20.4 %all_to_all.25 = bf16[2,32,3,1024]{3,0,2,1:T(2,128)(2,1)} all-to-all(bf16[2,32,3,1024]{3,0,2,1:T(2,128)(2,1)S(1)} %copy.132), channel_id=1, replica_groups=mesh['seq'=16,'exp'=32] {'exp'}, dimensions={1} | all-to-all | bytes 786432 | tf_op jit(solution)/shard_map/all_to_all | solution.py:49
  38.5 0.9 add_divide_fusion.1
  39.3 0.2 select_reduce_fusion
  39.6 0.2 fusion.9
  39.8 0.4 copy-done.37
  40.2 10.5 %all_to_all.26 = bf16[1,32,3]{2,0,1:T(2,128)(2,1)S(1)} all-to-all(bf16[1,32,3]{2,0,1:T(2,128)(2,1)S(1)} %reshape.729), channel_id=1, replica_groups=mesh['seq'=16,'exp'=32] {'exp'}, dimensions={1} | all-to-all | bytes 384 | tf_op jit(solution)/shard_map/all_to_all | solution.py:50
  50.7 33.3 %all_gather.6 = bf16[1,512,3]{2,0,1:T(2,128)(2,1)S(1)} all-gather(bf16[1,32,3]{2,0,1:T(2,128)(2,1)S(1)} %all_to_all.26), channel_id=1, replica_groups=mesh['seq'=16,'exp'=32] {'seq'}, dimensions={1}, use_global_device_ids=true | all-gather | bytes 3264 | tf_op jit(solution)/shard_map/all_gather | solution.py:54
  84.1 0.8 convert_reduce_fusion
  84.8 0.2 reshape.717
  85.0 38.5 %all-gather.2.cloned.1.call-done = bf16[2,512,3,1024]{3,0,2,1:T(2,128)(2,1)} async-done(((bf16[2,32,3,1024]{3,0,2,1:T(2,128)(2,1)}), bf16[2,512,3,1024]{3,0,2,1:T(2,128)(2,1)}) %all-gather.2.cloned.1.call-update) | async-done | bytes 6291472 | tf_op jit(solution)/shard_map/all_gather | solution.py:53
  123.6 34.7 %slice_reduce_fusion = (bf16[512,3,1024]{2,1,0:T(4,128)(2,1)}, bf16[512,3,1024]{2,1,0:T(4,128)(2,1)}) fusion(bf16[2,512,3,1024]{3,0,2,1:T(2,128)(2,1)} %all-gather.2.cloned.1.call-done), kind=kLoop, calls=%fused_computation | loop fusion | bytes 12582912 | tf_op jit(solution)/shard_map/slice | solution.py:102
  158.3 8.8 %reshape_squeeze.6 = bf16[1536,1024]{1,0:T(8,128)(2,1)} reshape(bf16[512,3,1024]{2,1,0:T(4,128)(2,1)} %get-tuple-element.4) | data formatting | bytes 6291456 | tf_op jit(solution)/shard_map/reshape;squeeze | solution.py:103
  167.1 8.9 %reshape_squeeze.7 = bf16[1536,1024]{1,0:T(8,128)(2,1)} reshape(bf16[512,3,1024]{2,1,0:T(4,128)(2,1)} %get-tuple-element.3) | data formatting | bytes 6291456 | tf_op jit(solution)/shard_map/reshape;squeeze | solution.py:102
  176.0 3.0 %fusion.18 = f32[1536,256]{0,1:T(8,128)S(1)} fusion(bf16[1536,1024]{1,0:T(8,128)(2,1)} %reshape_squeeze.6, bf16[1,256,1024]{2,1,0:T(8,128)(2,1)S(1)} %copy-done.50), kind=kOutput, calls=%fused_computation.34 | convolution fusion | flops 805306368 | bytes 5242880 | tf_op jit(solution)/shard_map/dot_general | solution.py:109
  179.1 3.4 %fusion.5 = (bf16[1536,256]{0,1:T(8,128)(2,1)S(1)}, f32[1536]{0:T(1024)}, f32[1536,256]{0,1:T(8,128)}) fusion(f32[1536,256]{0,1:T(8,128)S(1)} %fusion.18, f32[1536]{0:T(1024)S(1)} %reshape.717, bf16[1536,1024]{1,0:T(8,128)(2,1)S(1)} %copy-done.2, bf16[1,1024,256]{2,1,0:T(8,128)(2,1)S(1)} %copy-done), kind=kOutput, calls=%fused_computation.9 | convolution fusion | flops 810809856 | bytes 7614464 | tf_op jit(solution)/shard_map/dot_general | solution.py:105
  182.5 2.7 convolution_convert_fusion
  185.2 0.7 div.162
  185.9 0.7 mul.503
  186.6 0.6 mul.506
  187.2 0.6 mul.509
  187.8 0.4 broadcast_in_dim.102
  188.2 0.6 copy.134
  188.8 0.6 copy.139
  189.5 0.8 copy.135
  190.2 0.6 mul.500
  190.8 1.0 mul.511
  191.9 0.2 mul.512
  192.1 24.7 %psum.7 = bf16[1536]{0:T(1024)(128)(2,1)S(1)} all-reduce(f32[1536]{0:T(1024)S(1)} %copy-done.34), channel_id=1, replica_groups=mesh['seq'=16,'exp'=32] {'seq'}, use_global_device_ids=true, to_apply=%region_11.12 | all-reduce | flops 1536 | bytes 9216 | tf_op jit(solution)/shard_map/psum | solution.py:132
  216.9 0.7 all_to_all.20
  217.6 14.2 %all-to-all-start.3 = ((bf16[32,1,3]{2,1,0:T(2,128)(2,1)}), bf16[32,1,3]{2,1,0:T(2,128)(2,1)S(1)}, u32[]{:S(2)}, u32[]{:S(2)}) async-start(bf16[32,1,3]{2,1,0:T(2,128)(2,1)} %all_to_all.20), calls=%async_computation.4 | async-start | bytes 32768 | tf_op jit(solution)/shard_map/all_to_all | solution.py:144
  231.8 4.5 %convolution_bitcast_fusion = f32[1,256,1024]{2,1,0:T(8,128)} fusion(bf16[1536,1024]{1,0:T(8,128)(2,1)} %reshape_squeeze.6, f32[1536]{0:T(1024)S(1)} %copy-done.33, f32[1536,256]{0,1:T(8,128)} %get-tuple-element.27), kind=kOutput, calls=%fused_computation.13 | convolution fusion | flops 807665664 | bytes 5773312 | tf_op jit(solution)/shard_map/dot_general | solution.py:117
  236.4 2.0 convolution_bitcast_fusion.1
  238.4 0.3 all-to-all-done.3
  238.9 0.2 fusion.34
  239.3 12.9 %reduce-scatter.2.cloned.1.call-done = bf16[96,1024]{1,0:T(8,128)(2,1)} async-done(((bf16[1536,1024]{1,0:T(8,128)(2,1)}), bf16[96,1024]{1,0:T(8,128)(2,1)}) %reduce-scatter.2.cloned.1.call-update) | async-done | bytes 196624 | tf_op jit(solution)/shard_map/reduce_scatter | solution.py:124
  252.2 1.7 reshape.713
  253.9 16.5 %all-to-all-start.2 = ((bf16[32,3,1024]{2,1,0:T(4,128)(2,1)}), bf16[32,3,1024]{2,1,0:T(4,128)(2,1)S(1)}, u32[]{:S(2)}, u32[]{:S(2)}) async-start(bf16[32,3,1024]{2,1,0:T(4,128)(2,1)} %reshape.713), calls=%async_computation.3 | async-start | bytes 524288 | tf_op jit(solution)/shard_map/all_to_all | solution.py:137
  270.5 0.2 fusion.38
  270.7 8.6 %all-to-all-done.2 = bf16[32,3,1024]{2,1,0:T(4,128)(2,1)S(1)} async-done(((bf16[32,3,1024]{2,1,0:T(4,128)(2,1)}), bf16[32,3,1024]{2,1,0:T(4,128)(2,1)S(1)}, u32[]{:S(2)}, u32[]{:S(2)}) %all-to-all-start.2) | async-done | bytes 196640 | tf_op jit(solution)/shard_map/all_to_all | solution.py:137
  279.6 0.3 multiply_reduce_fusion.7
  280.0 0.5 multiply_reduce_fusion.2
  280.8 0.2 broadcast_in_dim.99
  281.0 0.4 multiply_reduce_fusion.5
  281.7 0.2 multiply_reduce_fusion.3
  282.0 0.2 multiply_add_fusion.1
  282.4 0.3 fusion.24
  282.7 0.3 broadcast_in_dim.108
  283.0 0.5 broadcast_in_dim.109
  283.6 0.3 fusion.20
  283.9 0.8 convert_element_type.81
  (150 shorter events, 3.9 us)
Async XLA Ops:
  7.2 171.9 %copy-start = (bf16[1,1024,256]{2,1,0:T(8,128)(2,1)S(1)}, bf16[1,1024,256]{2,1,0:T(8,128)(2,1)}, u32[]{:S(2)}) copy-start(bf16[1,1024,256]{2,1,0:T(8,128)(2,1)} %param.13) | copy-start | bytes 1572868
  7.2 2.6 copy-start.1
  7.2 116.4 %all-gather.2.cloned.1.call-start = ((), (), s32[]{:S(2)}) async-start(), calls=%async_computation.5 | async-start | bytes 6684672 | tf_op jit(solution)/shard_map/all_gather | solution.py:53
  8.6 2.3 copy-start.21
  11.7 2.1 copy-start.15
  12.0 3.0 %copy-start.4 = (f32[32,1024]{1,0:T(8,128)}, f32[32,1024]{1,0:T(8,128)S(1)}, u32[]{:S(2)}) copy-start(f32[32,1024]{1,0:T(8,128)S(1)} %broadcast_multiply_fusion.1) | copy-start | bytes 393220
  12.2 2.9 copy-start.35
  13.0 2.1 copy-start.17
  13.0 2.8 copy-start.26
  13.3 3.3 %copy-start.24 = (f32[1024]{0:T(1024)S(1)}, f32[1024]{0:T(1024)}, u32[]{:S(2)}) copy-start(f32[1024]{0:T(1024)} %param.10) | copy-start | bytes 12292
  13.8 3.5 %copy-start.13 = (bf16[1,32,1024]{2,1,0:T(8,128)(2,1)S(1)}, bf16[1,32,1024]{2,1,0:T(8,128)(2,1)}, u32[]{:S(2)}) copy-start(bf16[1,32,1024]{2,1,0:T(8,128)(2,1)} %param.15) | copy-start | bytes 196612
  13.9 172.0 %copy-start.7 = (f32[32,4]{1,0:T(8,128)}, f32[32,4]{1,0:T(8,128)S(1)}, u32[]{:S(2)}) copy-start(f32[32,4]{1,0:T(8,128)S(1)} %get-tuple-element.20) | copy-start | bytes 1540
  13.9 173.2 %copy-start.9 = (f32[32,4]{1,0:T(8,128)}, f32[32,4]{1,0:T(8,128)S(1)}, u32[]{:S(2)}) copy-start(f32[32,4]{1,0:T(8,128)S(1)} %get-tuple-element.22) | copy-start | bytes 1540
  15.2 0.6 copy-start.48
  16.5 23.0 %copy-start.40 = (s32[32,2]{0,1:T(2,128)}, s32[32,2]{0,1:T(2,128)S(1)}, u32[]{:S(2)}) copy-start(s32[32,2]{0,1:T(2,128)S(1)} %multiply_add_fusion.2) | copy-start | bytes 772
  16.6 1.3 copy-start.19
  17.1 21.3 %copy-start.11 = (bf16[1024,32]{0,1:T(8,128)(2,1)S(1)}, bf16[1024,32]{0,1:T(8,128)(2,1)}, u32[]{:S(2)}) copy-start(bf16[1024,32]{0,1:T(8,128)(2,1)} %param.11) | copy-start | bytes 196612
  38.4 213.8 %reduce-scatter.2.cloned.1.call-start = ((), (), s32[]{:S(2)}) async-start(), calls=%async_computation.6 | async-start | bytes 3342336 | tf_op jit(solution)/shard_map/reduce_scatter | solution.py:124
  39.5 0.6 copy-start.37
  39.5 118.8 %copy-start.28 = (f32[32,2]{0,1:T(2,128)}, f32[32,2]{0,1:T(2,128)S(1)}, u32[]{:S(2)}) copy-start(f32[32,2]{0,1:T(2,128)S(1)} %get-tuple-element.12) | copy-start | bytes 772
  85.0 94.0 %copy-start.32 = (f32[1536]{0:T(1024)}, f32[1536]{0:T(1024)S(1)}, u32[]{:S(2)}) copy-start(f32[1536]{0:T(1024)S(1)} %reshape.717) | copy-start | bytes 18436
  167.1 8.9 %copy-start.50 = (bf16[1,256,1024]{2,1,0:T(8,128)(2,1)S(1)}, bf16[1,256,1024]{2,1,0:T(8,128)(2,1)}, u32[]{:S(2)}) copy-start(bf16[1,256,1024]{2,1,0:T(8,128)(2,1)} %param.14) | copy-start | bytes 1572868
  176.0 3.1 %copy-start.2 = (bf16[1536,1024]{1,0:T(8,128)(2,1)S(1)}, bf16[1536,1024]{1,0:T(8,128)(2,1)}, u32[]{:S(2)}) copy-start(bf16[1536,1024]{1,0:T(8,128)(2,1)} %reshape_squeeze.7) | copy-start | bytes 9437188
  188.2 3.9 %copy-start.38 = (f32[32]{0:T(128)S(1)}, f32[32]{0:T(128)}, u32[]{:S(2)}) copy-start(f32[32]{0:T(128)} %copy-done.37) | copy-start | bytes 388
  188.2 3.9 %copy-start.34 = (f32[1536]{0:T(1024)S(1)}, f32[1536]{0:T(1024)}, u32[]{:S(2)}) copy-start(f32[1536]{0:T(1024)} %get-tuple-element.16) | copy-start | bytes 18436
  188.2 43.6 %copy-start.33 = (f32[1536]{0:T(1024)S(1)}, f32[1536]{0:T(1024)}, u32[]{:S(2)}) copy-start(f32[1536]{0:T(1024)} %copy-done.32) | copy-start | bytes 18436
  217.6 21.1 %all-to-all-start.3 = ((bf16[32,1,3]{2,1,0:T(2,128)(2,1)}), bf16[32,1,3]{2,1,0:T(2,128)(2,1)S(1)}, u32[]{:S(2)}, u32[]{:S(2)}) async-start(bf16[32,1,3]{2,1,0:T(2,128)(2,1)} %all_to_all.20), calls=%async_computation.4 | async-start | bytes 32768 | tf_op jit(solution)/shard_map/all_to_all | solution.py:144
  231.8 4.5 %copy-start.3 = (bf16[1536,1024]{1,0:T(8,128)(2,1)S(1)}, bf16[1536,1024]{1,0:T(8,128)(2,1)}, u32[]{:S(2)}) copy-start(bf16[1536,1024]{1,0:T(8,128)(2,1)} %reshape_squeeze.7) | copy-start | bytes 9437188
  236.3 2.6 copy-start.41
  236.3 2.8 copy-start.29
  236.3 2.9 copy-start.39
  236.3 2.9 copy-start.27
  236.3 34.1 %copy-start.12 = (bf16[1024,32]{0,1:T(8,128)(2,1)S(1)}, bf16[1024,32]{0,1:T(8,128)(2,1)}, u32[]{:S(2)}) copy-start(bf16[1024,32]{0,1:T(8,128)(2,1)} %param.11) | copy-start | bytes 196612
  236.3 34.1 %copy-start.23 = (f32[32,32]{1,0:T(8,128)S(1)}, f32[32,32]{1,0:T(8,128)}, u32[]{:S(2)}) copy-start(f32[32,32]{1,0:T(8,128)} %get-tuple-element.26) | copy-start | bytes 12292
  238.4 41.1 %copy-start.20 = (bf16[32,96]{1,0:T(8,128)(2,1)S(1)}, bf16[32,96]{1,0:T(8,128)(2,1)}, u32[]{:S(2)}) copy-start(bf16[32,96]{1,0:T(8,128)(2,1)} %copy-done.19) | copy-start | bytes 18436
  238.4 41.1 %copy-start.25 = (f32[1024]{0:T(1024)S(1)}, f32[1024]{0:T(1024)}, u32[]{:S(2)}) copy-start(f32[1024]{0:T(1024)} %param.10) | copy-start | bytes 12292
  238.4 41.5 %copy-start.49 = (f32[32]{0:T(128)S(1)}, f32[32]{0:T(128)}, u32[]{:S(2)}) copy-start(f32[32]{0:T(128)} %copy-done.48) | copy-start | bytes 388
  238.4 41.5 %copy-start.14 = (bf16[1,32,1024]{2,1,0:T(8,128)(2,1)S(1)}, bf16[1,32,1024]{2,1,0:T(8,128)(2,1)}, u32[]{:S(2)}) copy-start(bf16[1,32,1024]{2,1,0:T(8,128)(2,1)} %param.15) | copy-start | bytes 196612
  238.4 41.5 %copy-start.47 = (f32[32]{0:T(128)S(1)}, f32[32]{0:T(128)}, u32[]{:S(2)}) copy-start(f32[32]{0:T(128)} %get-tuple-element.23) | copy-start | bytes 388
  238.4 41.6 %copy-start.5 = (f32[32,1024]{1,0:T(8,128)S(1)}, f32[32,1024]{1,0:T(8,128)}, u32[]{:S(2)}) copy-start(f32[32,1024]{1,0:T(8,128)} %copy-done.4) | copy-start | bytes 393220
  238.4 41.6 %copy-start.10 = (f32[32,4]{1,0:T(8,128)S(1)}, f32[32,4]{1,0:T(8,128)}, u32[]{:S(2)}) copy-start(f32[32,4]{1,0:T(8,128)} %copy-done.9) | copy-start | bytes 1540
  253.9 25.4 %all-to-all-start.2 = ((bf16[32,3,1024]{2,1,0:T(4,128)(2,1)}), bf16[32,3,1024]{2,1,0:T(4,128)(2,1)S(1)}, u32[]{:S(2)}, u32[]{:S(2)}) async-start(bf16[32,3,1024]{2,1,0:T(4,128)(2,1)} %reshape.713), calls=%async_computation.3 | async-start | bytes 524288 | tf_op jit(solution)/shard_map/all_to_all | solution.py:137
  279.5 1.4 copy-start.42
  279.5 1.4 copy-start.43
  279.5 1.4 copy-start.44
  279.6 1.4 copy-start.45
  279.6 1.4 copy-start.46
  280.7 1.0 copy-start.6
  280.7 0.9 copy-start.30
  280.7 0.9 copy-start.31
  280.7 1.3 copy-start.16
  280.7 1.3 copy-start.18
  280.8 1.3 copy-start.36
  281.0 1.4 copy-start.22
  281.9 1.7 copy-start.8
Sparse Core Ops, SparseCore 0:
  38.5 85.0 all-gather.1
  185.3 66.7 reduce-scatter.1
where the time goes:
time: 292 us
  blocking collectives  88.9 us (30%)
  local copies, waits for them, and re-layouts  70.2 us (24%)
  waiting for transfers between devices  60.4 us (21%)
  starting transfers between devices  30.8 us (11%)
  matrix products  19.3 us (7%)
  between operations  15 us (5%)
  other arithmetic  6.98 us (2%)
    all_gather x1, waiting for transfers between devices, deliver(): lax.all_gather(owned_rows, 'seq', axis=1, tiled=True)  38.5 us
    slice x1, local copies, waits for them, and re-layouts, per_device(): token_rows = both_rows[0].reshape(slot_count, width_model)  34.7 us
    all_gather x1, blocking collectives, deliver(): lax.all_gather(owned_gates, 'seq', axis=1, tiled=True)  33.3 us
    psum x1, blocking collectives, per_device(): every_term = lax.psum(gate_terms, 'seq')  24.7 us
    all_to_all x1, blocking collectives, deliver(): lax.all_to_all(row_stack, 'exp', split_axis=1, concat_axis=1, tiled=True)  20.4 us
    all_to_all x1, starting transfers between devices, per_device(): lax.all_to_all(summed_rows.reshape(owners, capacity, width_model), 'exp',...  16.5 us
    all_to_all x1, starting transfers between devices, per_device(): lax.all_to_all(own_terms.astype(jnp.bfloat16).reshape(owners, capacity),...  14.2 us
    reduce_scatter x1, waiting for transfers between devices, per_device(): lax.psum_scatter(lax.dot_general(hidden_grad, weight_in, contract_cols, p...  12.9 us
  transfers between devices with their start and end apart: 4, of which 4 were waited for; matrix products, arithmetic and copies ran while one was open for 6% of the time, Pallas kernels for 0%

commit v1 on v0

--- a/solution.py
+++ b/solution.py
@@ -58,6 +58,16 @@
 def per_device(
     byte_embed, score_weight, norm_gain, router, routes, expert_in, expert_out, cotangent
 ):
+
+    def fill_the_desk(vector, along_axis):
+        nodes = lax.axis_size(along_axis)
+        shaped = vector
+        for c in [m for m in (1, 2, 4, 8, 16) if m < nodes]:
+            shaped = shaped + lax.ppermute(
+                shaped, axis_name=along_axis, perm=tuple(((ix, ix ^ c) for ix in range(nodes)))
+            )
+        return shaped
+
     experts_all = router.shape[1]
     token_count = routes.shape[1]
     width_model = byte_embed.shape[2]
@@ -129,7 +139,7 @@
         scatter_dimension=0,
         tiled=True,
     )
-    every_term = lax.psum(gate_terms, "seq")
+    every_term = fill_the_desk(gate_terms, "seq")
     own_terms = lax.dynamic_slice_in_dim(
         every_term, lax.axis_index("seq") * own_slots, own_slots, 0
     )

time: 292 us -> 293 us (level)
  blocking collectives: 88.9 us -> 64.4 us
  starting transfers between devices: 30.8 us -> 47 us
  waiting for transfers between devices: 60.4 us -> 65.2 us
  other arithmetic: 6.98 us -> 10.2 us
    psum x1 -> x0, blocking collectives: 24.7 us -> none  [per_device(): every_term = lax.psum(gate_terms, 'seq')]
    ppermute x0 -> x4, starting transfers between devices: none -> 19.2 us  [fill_the_desk(): lax.ppermute(shaped, axis_name=along_axis, perm=tuple(((ix, ix ^ c) for i...]
    ppermute x0 -> x4, waiting for transfers between devices: none -> 5.89 us  [fill_the_desk(): lax.ppermute(shaped, axis_name=along_axis, perm=tuple(((ix, ix ^ c) for i...]
    reduce_scatter x1, waiting for transfers between devices: 12.9 us -> 9.1 us  [per_device(): lax.psum_scatter(lax.dot_general(hidden_grad, weight_in, contract_cols, p...]
    all_to_all x1, starting transfers between devices: 14.2 us -> 11.2 us  [per_device(): lax.all_to_all(own_terms.astype(jnp.bfloat16).reshape(owners, capacity),...]
  transfers between devices with their start and end apart: 4 -> 8, of which waited for: 4 -> 7; matrix products, arithmetic and copies ran while one was open for 6% -> 7% of each run, Pallas kernels for 0% -> 0%
where the time goes in v1:
time: 293 us; the launch traced here: 292 us
  local copies, waits for them, and re-layouts  69.8 us (24%)
  waiting for transfers between devices  65.2 us (22%)
  blocking collectives  64.4 us (22%)
  starting transfers between devices  47 us (16%)
  matrix products  20.5 us (7%)
  between operations  14.9 us (5%)
  other arithmetic  10.2 us (3%)
    all_gather x1, waiting for transfers between devices, deliver(): lax.all_gather(owned_rows, 'seq', axis=1, tiled=True)  38.7 us
    slice x1, local copies, waits for them, and re-layouts, per_device(): token_rows = both_rows[0].reshape(slot_count, width_model)  34.7 us
    all_gather x1, blocking collectives, deliver(): lax.all_gather(owned_gates, 'seq', axis=1, tiled=True)  33.5 us
    all_to_all x1, blocking collectives, deliver(): lax.all_to_all(row_stack, 'exp', split_axis=1, concat_axis=1, tiled=True)  20.4 us
    ppermute x4, starting transfers between devices, fill_the_desk(): lax.ppermute(shaped, axis_name=along_axis, perm=tuple(((ix, ix ^ c) for i...  19.2 us
    all_to_all x1, starting transfers between devices, per_device(): lax.all_to_all(summed_rows.reshape(owners, capacity, width_model), 'exp',...  16.6 us
    all_to_all x1, starting transfers between devices, per_device(): lax.all_to_all(own_terms.astype(jnp.bfloat16).reshape(owners, capacity),...  11.2 us
    all_to_all x1, blocking collectives, deliver(): lax.all_to_all(gates_in, 'exp', split_axis=1, concat_axis=1, tiled=True)  10.5 us
  transfers between devices with their start and end apart: 8, of which 7 were waited for; matrix products, arithmetic and copies ran while one was open for 7% of the time, Pallas kernels for 0%

profile of v1, /device:TPU:1, one launch (start us, length us, event | category | flops | bytes accessed | tf_op | source)
XLA Modules:
  0.0 292.1 jit_solution(10904065505559599057)
XLA Ops:
  7.2 1.4 reshape.708
  8.6 1.1 reshape.709
  10.0 0.8 reduce_sum.182
  11.0 0.6 fusion.54
  11.7 0.3 reduce_sum.183
  12.2 0.7 fusion.22
  13.0 0.3 broadcast_in_dim.93
  13.3 0.5 broadcast_in_dim.94
  13.9 1.1 fusion.21
  15.2 0.6 fusion.50
  16.7 0.3 convolution_convert_fusion.2
  17.6 0.4 copy.132
  18.0 20.4 %all_to_all.25 = bf16[2,32,3,1024]{3,0,2,1:T(2,128)(2,1)} all-to-all(bf16[2,32,3,1024]{3,0,2,1:T(2,128)(2,1)S(1)} %copy.132), channel_id=1, replica_groups=mesh['seq'=16,'exp'=32] {'exp'}, dimensions={1} | all-to-all | bytes 786432 | tf_op jit(solution)/shard_map/all_to_all | solution.py:49
  38.5 0.9 add_divide_fusion.1
  39.4 0.2 select_reduce_fusion
  39.9 10.5 %all_to_all.26 = bf16[1,32,3]{2,0,1:T(2,128)(2,1)S(1)} all-to-all(bf16[1,32,3]{2,0,1:T(2,128)(2,1)S(1)} %reshape.729), channel_id=1, replica_groups=mesh['seq'=16,'exp'=32] {'exp'}, dimensions={1} | all-to-all | bytes 384 | tf_op jit(solution)/shard_map/all_to_all | solution.py:50
  50.4 33.5 %all_gather.6 = bf16[1,512,3]{2,0,1:T(2,128)(2,1)S(1)} all-gather(bf16[1,32,3]{2,0,1:T(2,128)(2,1)S(1)} %all_to_all.26), channel_id=1, replica_groups=mesh['seq'=16,'exp'=32] {'seq'}, dimensions={1}, use_global_device_ids=true | all-gather | bytes 3264 | tf_op jit(solution)/shard_map/all_gather | solution.py:54
  83.9 0.8 convert_reduce_fusion
  84.7 0.2 reshape.717
  84.9 38.7 %all-gather.2.cloned.1.call-done = bf16[2,512,3,1024]{3,0,2,1:T(2,128)(2,1)} async-done(((bf16[2,32,3,1024]{3,0,2,1:T(2,128)(2,1)}), bf16[2,512,3,1024]{3,0,2,1:T(2,128)(2,1)}) %all-gather.2.cloned.1.call-update) | async-done | bytes 6291472 | tf_op jit(solution)/shard_map/all_gather | solution.py:53
  123.6 34.7 %slice_reduce_fusion = (bf16[512,3,1024]{2,1,0:T(4,128)(2,1)}, bf16[512,3,1024]{2,1,0:T(4,128)(2,1)}) fusion(bf16[2,512,3,1024]{3,0,2,1:T(2,128)(2,1)} %all-gather.2.cloned.1.call-done), kind=kLoop, calls=%fused_computation | loop fusion | bytes 12582912 | tf_op jit(solution)/shard_map/slice | solution.py:112
  158.3 8.8 %reshape_squeeze.6 = bf16[1536,1024]{1,0:T(8,128)(2,1)} reshape(bf16[512,3,1024]{2,1,0:T(4,128)(2,1)} %get-tuple-element.4) | data formatting | bytes 6291456 | tf_op jit(solution)/shard_map/reshape;squeeze | solution.py:113
  167.1 8.9 %reshape_squeeze.7 = bf16[1536,1024]{1,0:T(8,128)(2,1)} reshape(bf16[512,3,1024]{2,1,0:T(4,128)(2,1)} %get-tuple-element.3) | data formatting | bytes 6291456 | tf_op jit(solution)/shard_map/reshape;squeeze | solution.py:112
  176.0 3.0 %fusion.18 = f32[1536,256]{0,1:T(8,128)S(1)} fusion(bf16[1536,1024]{1,0:T(8,128)(2,1)} %reshape_squeeze.6, bf16[1,256,1024]{2,1,0:T(8,128)(2,1)S(1)} %copy-done.43), kind=kOutput, calls=%fused_computation.34 | convolution fusion | flops 805306368 | bytes 5242880 | tf_op jit(solution)/shard_map/dot_general | solution.py:119
  179.1 2.8 fusion.5
  181.9 2.7 convolution_convert_fusion
  184.6 1.9 collective-permute-start
  186.5 2.5 collective-permute-done
  189.0 2.4 collective-permute-start.1
  191.4 2.9 collective-permute-done.1
  194.3 0.6 add.109
  194.9 6.4 %collective-permute-start.2 = (f32[1536]{0:T(1024)}, f32[1536]{0:T(1024)}, u32[]{:S(2)}, u32[]{:S(2)}) collective-permute-start(f32[1536]{0:T(1024)} %add.109), channel_id=1, source_target_pairs={{0,128},{32,160},{64,192},{96,224},{128,0},{160,32},{192,64},{224,... | collective-permute-start | bytes 18440 | tf_op jit(solution)/shard_map/ppermute | solution.py:66
  201.3 0.5 multiply_divide_fusion.1
  201.8 0.7 div.162
  202.5 0.6 mul.503
  203.1 0.7 mul.506
  203.8 0.6 mul.509
  204.4 0.4 broadcast_in_dim.102
  204.8 0.7 copy.134
  205.5 0.6 copy.139
  206.1 0.8 copy.135
  206.9 0.6 mul.500
  207.5 1.0 mul.511
  208.8 0.7 add.110
  209.5 8.5 %collective-permute-start.3 = (f32[1536]{0:T(1024)S(1)}, f32[1536]{0:T(1024)S(1)}, u32[]{:S(2)}, u32[]{:S(2)}) collective-permute-start(f32[1536]{0:T(1024)S(1)} %add.110), channel_id=1, source_target_pairs={{0,256},{32,288},{64,320},{96,352},{128,384},{160,416},{192,448},{... | collective-permute-start | bytes 18440 | tf_op jit(solution)/shard_map/ppermute | solution.py:66
  218.0 4.4 %convolution_bitcast_fusion = f32[1,256,1024]{2,1,0:T(8,128)} fusion(bf16[1536,1024]{1,0:T(8,128)(2,1)} %reshape_squeeze.6, f32[1536]{0:T(1024)} %copy-done.32, f32[1536,256]{0,1:T(8,128)} %get-tuple-element.27), kind=kOutput, calls=%fused_computation.13 | convolution fusion | flops 807665664 | bytes 5773312 | tf_op jit(solution)/shard_map/dot_general | solution.py:127
  222.4 0.5 collective-permute-done.3
  223.0 0.7 all_to_all.20
  223.7 11.2 %all-to-all-start.3 = ((bf16[32,1,3]{2,1,0:T(2,128)(2,1)}), bf16[32,1,3]{2,1,0:T(2,128)(2,1)S(1)}, u32[]{:S(2)}, u32[]{:S(2)}) async-start(bf16[32,1,3]{2,1,0:T(2,128)(2,1)} %all_to_all.20), calls=%async_computation.4 | async-start | bytes 32768 | tf_op jit(solution)/shard_map/all_to_all | solution.py:154
  235.0 3.9 %convolution_bitcast_fusion.1 = f32[1,1024,256]{2,1,0:T(8,128)} fusion(bf16[1536,1024]{1,0:T(8,128)(2,1)} %reshape_squeeze.7, bf16[1536,256]{0,1:T(8,128)(2,1)S(1)} %get-tuple-element.15), kind=kOutput, calls=%fused_computation.14 | convolution fusion | flops 805306368 | bytes 4980736 | tf_op jit(solution)/shard_map/dot_general | solution.py:130
  239.0 2.9 all-to-all-done.3
  242.4 9.1 %reduce-scatter.2.cloned.1.call-done = bf16[96,1024]{1,0:T(8,128)(2,1)} async-done(((bf16[1536,1024]{1,0:T(8,128)(2,1)}), bf16[96,1024]{1,0:T(8,128)(2,1)}) %reduce-scatter.2.cloned.1.call-update) | async-done | bytes 196624 | tf_op jit(solution)/shard_map/reduce_scatter | solution.py:134
  251.5 1.7 reshape.713
  253.3 16.6 %all-to-all-start.2 = ((bf16[32,3,1024]{2,1,0:T(4,128)(2,1)}), bf16[32,3,1024]{2,1,0:T(4,128)(2,1)S(1)}, u32[]{:S(2)}, u32[]{:S(2)}) async-start(bf16[32,3,1024]{2,1,0:T(4,128)(2,1)} %reshape.713), calls=%async_computation.3 | async-start | bytes 524288 | tf_op jit(solution)/shard_map/all_to_all | solution.py:147
  270.1 8.6 %all-to-all-done.2 = bf16[32,3,1024]{2,1,0:T(4,128)(2,1)S(1)} async-done(((bf16[32,3,1024]{2,1,0:T(4,128)(2,1)}), bf16[32,3,1024]{2,1,0:T(4,128)(2,1)S(1)}, u32[]{:S(2)}, u32[]{:S(2)}) %all-to-all-start.2) | async-done | bytes 196640 | tf_op jit(solution)/shard_map/all_to_all | solution.py:147
  278.9 0.3 multiply_reduce_fusion.7
  279.4 1.1 multiply_reduce_fusion.2
  280.9 1.1 multiply_reduce_fusion.5
  282.2 0.2 multiply_reduce_fusion.3
  283.0 0.3 fusion.24
  283.3 0.3 broadcast_in_dim.108
  283.6 0.5 broadcast_in_dim.109
  284.2 0.3 fusion.20
  284.5 0.8 convert_element_type.81
  (146 shorter events, 5.3 us)
Async XLA Ops:
  7.2 171.9 %copy-start = (bf16[1,1024,256]{2,1,0:T(8,128)(2,1)S(1)}, bf16[1,1024,256]{2,1,0:T(8,128)(2,1)}, u32[]{:S(2)}) copy-start(bf16[1,1024,256]{2,1,0:T(8,128)(2,1)} %param.13) | copy-start | bytes 1572868
  7.2 2.6 copy-start.1
  7.2 116.4 %all-gather.2.cloned.1.call-start = ((), (), s32[]{:S(2)}) async-start(), calls=%async_computation.5 | async-start | bytes 6684672 | tf_op jit(solution)/shard_map/all_gather | solution.py:53
  8.6 2.3 copy-start.20
  11.7 2.1 copy-start.14
  12.0 3.0 %copy-start.3 = (f32[32,1024]{1,0:T(8,128)}, f32[32,1024]{1,0:T(8,128)S(1)}, u32[]{:S(2)}) copy-start(f32[32,1024]{1,0:T(8,128)S(1)} %broadcast_multiply_fusion.1) | copy-start | bytes 393220
  12.2 2.9 copy-start.33
  13.0 2.1 copy-start.16
  13.0 2.8 copy-start.26
  13.3 3.4 %copy-start.24 = (f32[1024]{0:T(1024)S(1)}, f32[1024]{0:T(1024)}, u32[]{:S(2)}) copy-start(f32[1024]{0:T(1024)} %param.10) | copy-start | bytes 12292
  13.8 3.5 %copy-start.12 = (bf16[1,32,1024]{2,1,0:T(8,128)(2,1)S(1)}, bf16[1,32,1024]{2,1,0:T(8,128)(2,1)}, u32[]{:S(2)}) copy-start(bf16[1,32,1024]{2,1,0:T(8,128)(2,1)} %param.15) | copy-start | bytes 196612
  13.9 188.6 %copy-start.6 = (f32[32,4]{1,0:T(8,128)}, f32[32,4]{1,0:T(8,128)S(1)}, u32[]{:S(2)}) copy-start(f32[32,4]{1,0:T(8,128)S(1)} %get-tuple-element.20) | copy-start | bytes 1540
  13.9 189.9 %copy-start.8 = (f32[32,4]{1,0:T(8,128)}, f32[32,4]{1,0:T(8,128)S(1)}, u32[]{:S(2)}) copy-start(f32[32,4]{1,0:T(8,128)S(1)} %get-tuple-element.22) | copy-start | bytes 1540
  15.2 0.6 copy-start.40
  16.6 23.0 %copy-start.37 = (s32[32,2]{0,1:T(2,128)}, s32[32,2]{0,1:T(2,128)S(1)}, u32[]{:S(2)}) copy-start(s32[32,2]{0,1:T(2,128)S(1)} %multiply_add_fusion.2) | copy-start | bytes 772
  16.7 1.3 copy-start.18
  17.2 21.3 %copy-start.10 = (bf16[1024,32]{0,1:T(8,128)(2,1)S(1)}, bf16[1024,32]{0,1:T(8,128)(2,1)}, u32[]{:S(2)}) copy-start(bf16[1024,32]{0,1:T(8,128)(2,1)} %param.11) | copy-start | bytes 196612
  38.4 213.1 %reduce-scatter.2.cloned.1.call-start = ((), (), s32[]{:S(2)}) async-start(), calls=%async_computation.6 | async-start | bytes 3342336 | tf_op jit(solution)/shard_map/reduce_scatter | solution.py:134
  39.6 118.7 %copy-start.28 = (f32[32,2]{0,1:T(2,128)}, f32[32,2]{0,1:T(2,128)S(1)}, u32[]{:S(2)}) copy-start(f32[32,2]{0,1:T(2,128)S(1)} %get-tuple-element.12) | copy-start | bytes 772
  39.6 161.7 %copy-start.35 = (f32[32]{0:T(128)}, f32[32]{0:T(128)S(1)}, u32[]{:S(2)}) copy-start(f32[32]{0:T(128)S(1)} %get-tuple-element.11) | copy-start | bytes 388
  84.9 94.2 %copy-start.32 = (f32[1536]{0:T(1024)}, f32[1536]{0:T(1024)S(1)}, u32[]{:S(2)}) copy-start(f32[1536]{0:T(1024)S(1)} %reshape.717) | copy-start | bytes 18436
  167.1 8.9 %copy-start.43 = (bf16[1,256,1024]{2,1,0:T(8,128)(2,1)S(1)}, bf16[1,256,1024]{2,1,0:T(8,128)(2,1)}, u32[]{:S(2)}) copy-start(bf16[1,256,1024]{2,1,0:T(8,128)(2,1)} %param.14) | copy-start | bytes 1572868
  176.0 3.1 %copy-start.2 = (bf16[1536,1024]{1,0:T(8,128)(2,1)S(1)}, bf16[1536,1024]{1,0:T(8,128)(2,1)}, u32[]{:S(2)}) copy-start(bf16[1536,1024]{1,0:T(8,128)(2,1)} %reshape_squeeze.7) | copy-start | bytes 9437188
  184.6 4.4 %collective-permute-start = (f32[1536]{0:T(1024)S(1)}, f32[1536]{0:T(1024)S(1)}, u32[]{:S(2)}, u32[]{:S(2)}) collective-permute-start(f32[1536]{0:T(1024)S(1)} %get-tuple-element.16), channel_id=1, source_target_pairs={{0,32},{32,0},{64,96},{96,64},{128,160},{160,128},{192,224},{224,1... | collective-permute-start | bytes 18440 | tf_op jit(solution)/shard_map/ppermute | solution.py:66
  189.0 5.3 %collective-permute-start.1 = (f32[1536]{0:T(1024)S(1)}, f32[1536]{0:T(1024)S(1)}, u32[]{:S(2)}, u32[]{:S(2)}) collective-permute-start(f32[1536]{0:T(1024)S(1)} %add.108), channel_id=1, source_target_pairs={{0,64},{32,96},{64,0},{96,32},{128,192},{160,224},{192,128},{224,1... | collective-permute-start | bytes 18440 | tf_op jit(solution)/shard_map/ppermute | solution.py:66
  194.9 13.9 %collective-permute-start.2 = (f32[1536]{0:T(1024)}, f32[1536]{0:T(1024)}, u32[]{:S(2)}, u32[]{:S(2)}) collective-permute-start(f32[1536]{0:T(1024)} %add.109), channel_id=1, source_target_pairs={{0,128},{32,160},{64,192},{96,224},{128,0},{160,32},{192,64},{224,... | collective-permute-start | bytes 18440 | tf_op jit(solution)/shard_map/ppermute | solution.py:66
  209.5 13.4 %collective-permute-start.3 = (f32[1536]{0:T(1024)S(1)}, f32[1536]{0:T(1024)S(1)}, u32[]{:S(2)}, u32[]{:S(2)}) collective-permute-start(f32[1536]{0:T(1024)S(1)} %add.110), channel_id=1, source_target_pairs={{0,256},{32,288},{64,320},{96,352},{128,384},{160,416},{192,448},{... | collective-permute-start | bytes 18440 | tf_op jit(solution)/shard_map/ppermute | solution.py:66
  223.7 18.2 %all-to-all-start.3 = ((bf16[32,1,3]{2,1,0:T(2,128)(2,1)}), bf16[32,1,3]{2,1,0:T(2,128)(2,1)S(1)}, u32[]{:S(2)}, u32[]{:S(2)}) async-start(bf16[32,1,3]{2,1,0:T(2,128)(2,1)} %all_to_all.20), calls=%async_computation.4 | async-start | bytes 32768 | tf_op jit(solution)/shard_map/all_to_all | solution.py:154
  234.9 7.1 %copy-start.38 = (s32[32,2]{0,1:T(2,128)S(1)}, s32[32,2]{0,1:T(2,128)}, u32[]{:S(2)}) copy-start(s32[32,2]{0,1:T(2,128)} %copy-done.37) | copy-start | bytes 772
  234.9 7.3 %copy-start.29 = (f32[32,2]{0,1:T(2,128)S(1)}, f32[32,2]{0,1:T(2,128)}, u32[]{:S(2)}) copy-start(f32[32,2]{0,1:T(2,128)} %copy-done.28) | copy-start | bytes 772
  234.9 7.3 %copy-start.42 = (f32[32]{0:T(128)S(1)}, f32[32]{0:T(128)}, u32[]{:S(2)}) copy-start(f32[32]{0:T(128)} %multiply_divide_fusion.1) | copy-start | bytes 388
  234.9 7.4 %copy-start.36 = (f32[32]{0:T(128)S(1)}, f32[32]{0:T(128)}, u32[]{:S(2)}) copy-start(f32[32]{0:T(128)} %copy-done.35) | copy-start | bytes 388
  234.9 7.4 %copy-start.27 = (s32[1,32,2]{1,2,0:T(2,128)S(1)}, s32[1,32,2]{1,2,0:T(2,128)}, u32[]{:S(2)}) copy-start(s32[1,32,2]{1,2,0:T(2,128)} %param.12) | copy-start | bytes 772
  234.9 34.9 %copy-start.11 = (bf16[1024,32]{0,1:T(8,128)(2,1)S(1)}, bf16[1024,32]{0,1:T(8,128)(2,1)}, u32[]{:S(2)}) copy-start(bf16[1024,32]{0,1:T(8,128)(2,1)} %param.11) | copy-start | bytes 196612
  235.0 34.9 %copy-start.22 = (f32[32,32]{1,0:T(8,128)S(1)}, f32[32,32]{1,0:T(8,128)}, u32[]{:S(2)}) copy-start(f32[32,32]{1,0:T(8,128)} %get-tuple-element.26) | copy-start | bytes 12292
  238.9 40.0 %copy-start.19 = (bf16[32,96]{1,0:T(8,128)(2,1)S(1)}, bf16[32,96]{1,0:T(8,128)(2,1)}, u32[]{:S(2)}) copy-start(bf16[32,96]{1,0:T(8,128)(2,1)} %copy-done.18) | copy-start | bytes 18436
  238.9 40.0 %copy-start.25 = (f32[1024]{0:T(1024)S(1)}, f32[1024]{0:T(1024)}, u32[]{:S(2)}) copy-start(f32[1024]{0:T(1024)} %param.10) | copy-start | bytes 12292
  238.9 40.3 %copy-start.41 = (f32[32]{0:T(128)S(1)}, f32[32]{0:T(128)}, u32[]{:S(2)}) copy-start(f32[32]{0:T(128)} %copy-done.40) | copy-start | bytes 388
  238.9 40.3 %copy-start.13 = (bf16[1,32,1024]{2,1,0:T(8,128)(2,1)S(1)}, bf16[1,32,1024]{2,1,0:T(8,128)(2,1)}, u32[]{:S(2)}) copy-start(bf16[1,32,1024]{2,1,0:T(8,128)(2,1)} %param.15) | copy-start | bytes 196612
  238.9 40.3 %copy-start.39 = (f32[32]{0:T(128)S(1)}, f32[32]{0:T(128)}, u32[]{:S(2)}) copy-start(f32[32]{0:T(128)} %get-tuple-element.23) | copy-start | bytes 388
  238.9 40.4 %copy-start.4 = (f32[32,1024]{1,0:T(8,128)S(1)}, f32[32,1024]{1,0:T(8,128)}, u32[]{:S(2)}) copy-start(f32[32,1024]{1,0:T(8,128)} %copy-done.3) | copy-start | bytes 393220
  238.9 40.4 %copy-start.9 = (f32[32,4]{1,0:T(8,128)S(1)}, f32[32,4]{1,0:T(8,128)}, u32[]{:S(2)}) copy-start(f32[32,4]{1,0:T(8,128)} %copy-done.8) | copy-start | bytes 1540
  253.3 25.5 %all-to-all-start.2 = ((bf16[32,3,1024]{2,1,0:T(4,128)(2,1)}), bf16[32,3,1024]{2,1,0:T(4,128)(2,1)S(1)}, u32[]{:S(2)}, u32[]{:S(2)}) async-start(bf16[32,3,1024]{2,1,0:T(4,128)(2,1)} %reshape.713), calls=%async_computation.3 | async-start | bytes 524288 | tf_op jit(solution)/shard_map/all_to_all | solution.py:147
  280.7 1.6 copy-start.5
  280.7 1.6 copy-start.30
  280.7 1.6 copy-start.31
  280.7 1.9 copy-start.15
  280.7 1.9 copy-start.17
  280.7 1.9 copy-start.23
  280.7 1.9 copy-start.34
  280.9 2.1 copy-start.21
  282.5 1.7 copy-start.7
Sparse Core Ops, SparseCore 0:
  38.5 84.9 all-gather.1
  184.7 66.7 reduce-scatter.1
